TPU v7x, 128 devices: a whole 4x4x4 slice. The times are simulated.
128 devices in a mesh: row: 16 (over y_hi, x, core), col: 8 (over z, y_lo).
Axes of the slice: x: 4, y: 4 (y_hi: 2, y_lo: 2; y = y_hi * 2 + y_lo), z: 4, core: 2. Of those that a mesh axis runs over, the one named last changes fastest.
Arguments:
- orbitals_in: float32 [16384, 256], P(('row', 'col')), may hold values from -6 to 6
- hblocks: bfloat16 [256, 128, 4096], P('row', 'col'), may hold values from -0.046875 to 0.046875
- block_cols: int32 [256, 128], P('row', 'col'), may hold values from 0 to 31, as said below
- live_counts: int32 [256, 8], P('row', 'col'), may hold values from 0 to 16, as said below
- onsite: bfloat16 [256, 4096], P(('row', 'col')), may hold values from -3 to 1, as said below
- cut_low: float32 [1], replicated, may hold values from -1.6 to -1
- top_bound: float32 [1], replicated, may hold values from 2.4 to 3.2
Outputs:
- orbitals: float32 [16384, 256], P(('row', 'col'))
- projected: float32 [256, 256], replicated
Inputs may be any that keep to these rules, and one draw needn't show every extreme that they name: `block_cols`: in block row b and column group c the first live_counts[b, c] slots name distinct block columns whose global block index exceeds b (strict upper triangle); the other slots are padding and are ignored. `live_counts`: block row 0 fills all 16 slots of every column group; the last block row has no live slot. `onsite`: every block is symmetric.
All inputs are finite; a program needn't handle non-finite values.
Results may differ from a plain program's by a relative error of at most 0.0008.
The roundings to bfloat16 on the way count: a program that leaves them out, or rounds other values in their place, can miss the bound.
Values may be sent and summed in bfloat16 or wider, within the bound.
A program may use at most 128 MiB of HBM per device.

v0:
```python
import jax
import jax.numpy as jnp
from jax import lax
from jax.sharding import PartitionSpec as P

BS = 64
K = 256
PB = 2
DEG = 3


def add_columns(dense_tile, portion):
    return jnp.dot(dense_tile, portion, preferred_element_type=jnp.float32)


def mirror_rows(dense_tile, row_set):
    return lax.dot_general(
        dense_tile, row_set, (((0,), (0,)), ((), ())), preferred_element_type=jnp.float32
    )


def build_tile(hblocks, block_cols, live_counts, column_blocks):
    row_blocks, slot_count, _ = hblocks.shape
    occupied = jnp.arange(slot_count, dtype=jnp.int32)[None, :] < live_counts
    selector = (
        block_cols[:, :, None] == jnp.arange(column_blocks, dtype=jnp.int32)[None, None, :]
    ) & occupied[:, :, None]
    blocks = hblocks.reshape(row_blocks, slot_count, BS, BS)
    dense_tile = jnp.einsum(
        "isc,isab->iacb", selector.astype(jnp.bfloat16), blocks, preferred_element_type=jnp.float32
    )
    return dense_tile.astype(jnp.bfloat16).reshape(row_blocks * BS, column_blocks * BS)


def local(orbitals_in, hblocks, block_cols, live_counts, onsite, cut_low, top_bound):
    row_devices = lax.axis_size("row")
    col_devices = lax.axis_size("col")
    column_blocks = row_devices * PB
    local_rows = PB * BS
    total_rows = row_devices * col_devices * local_rows
    dense_tile = build_tile(hblocks, block_cols, live_counts, column_blocks)
    onsite_blocks = onsite.reshape(PB, BS, BS)

    def reduce_direct(terms):
        return lax.psum_scatter(terms, "col", scatter_dimension=0, tiled=True)

    def apply(rounded):
        onsite_part = jnp.einsum(
            "pab,pbk->pak",
            onsite_blocks,
            rounded.reshape(PB, BS, K),
            preferred_element_type=jnp.float32,
        ).reshape(local_rows, K)
        direct = reduce_direct(
            add_columns(dense_tile, lax.all_gather(rounded, "row", axis=0, tiled=True))
        )
        mirror = lax.psum_scatter(
            mirror_rows(dense_tile, lax.all_gather(rounded, "col", axis=0, tiled=True)),
            "row",
            scatter_dimension=0,
            tiled=True,
        )
        return onsite_part + direct + mirror

    centre = 0.5 * (top_bound[0] + cut_low[0])
    halfwidth = 0.5 * (top_bound[0] - cut_low[0])
    previous = orbitals_in
    current = (apply(orbitals_in.astype(jnp.bfloat16)) - centre * orbitals_in) / halfwidth
    for degree in range(DEG - 1):
        following = (
            2.0 * (apply(current.astype(jnp.bfloat16)) - centre * current) / halfwidth - previous
        )
        previous, current = (current, following)
    rounded = current.astype(jnp.bfloat16)
    as_float = rounded.astype(jnp.float32)
    contract = (((0,), (0,)), ((), ()))
    gram_part = lax.dot_general(rounded, rounded, contract, preferred_element_type=jnp.float32)
    image = apply(rounded)
    cross_part = lax.dot_general(as_float, image, contract, precision=lax.Precision.HIGHEST)
    gram_total, cross_total = lax.psum((gram_part, cross_part), ("row", "col"))
    gram_matrix = gram_total / total_rows
    ritz_matrix = (cross_total + cross_total.T) / (2.0 * total_rows)
    factor = jnp.linalg.cholesky(gram_matrix)
    orbitals = jax.scipy.linalg.solve_triangular(factor, current.T, lower=True).T
    inner = jax.scipy.linalg.solve_triangular(factor, ritz_matrix, lower=True)
    projected = jax.scipy.linalg.solve_triangular(factor, inner.T, lower=True)
    return (orbitals, projected)


def solution(mesh):
    placed = (
        P(("row", "col"), None),
        P("row", "col", None),
        P("row", "col"),
        P("row", "col"),
        P(("row", "col"), None),
        P(),
        P(),
    )
    return jax.shard_map(
        local, mesh=mesh, in_specs=placed, out_specs=(P(("row", "col"), None), P()), check_vma=False
    )
```

profile of v0, /device:TPU:1, one launch (start us, length us, event | category | flops | bytes accessed | tf_op | source)
XLA Modules:
  0.0 903.4 jit_solution(17615895773485688638)
XLA Ops:
  7.2 1.5 convert_element_type.20
  8.8 6.9 reshape.92
  15.8 8.9 convert_bitcast_fusion
  24.7 12.4 %reshape.93 = bf16[1024,2048]{1,0:T(8,128)(2,1)} reshape(bf16[16,64,32,64]{3,2,1,0:T(8,128)(2,1)} %convert_bitcast_fusion) | data formatting | bytes 8388608 | tf_op jit(solution)/shard_map/reshape | solution.py:32
  37.1 29.5 %all_gather.25 = bf16[1024,256]{1,0:T(8,128)(2,1)S(1)} all-gather(bf16[128,256]{1,0:T(8,128)(2,1)S(1)} %copy-done.2), channel_id=1, replica_groups=mesh['row'=16,'col'=8] {'col'}, dimensions={0}, use_global_device_ids=true | all-gather | bytes 589824 | tf_op jit(solution)/shard_map/all_gather | solution.py:58
  66.6 4.8 fusion.46
  71.6 4.7 fusion.45
  77.9 67.4 %reduce-scatter.11.cloned.1.call-done = f32[128,256]{1,0:T(8,128)} async-done(((f32[2048,256]{1,0:T(8,128)}), f32[128,256]{1,0:T(8,128)}) %reduce-scatter.11.cloned.1.call-update) | async-done | bytes 131088 | tf_op jit(solution)/shard_map/reduce_scatter | solution.py:57
  145.3 39.7 %reduce-scatter.9.cloned.1.call-done = f32[128,256]{1,0:T(8,128)} async-done(((f32[1024,256]{1,0:T(8,128)}), f32[128,256]{1,0:T(8,128)}) %reduce-scatter.9.cloned.1.call-update) | async-done | bytes 131088 | tf_op jit(solution)/shard_map/reduce_scatter | solution.py:45
  185.0 1.6 fusion.41
  186.7 23.9 %all_gather.27 = bf16[1024,256]{1,0:T(8,128)(2,1)S(1)} all-gather(bf16[128,256]{1,0:T(8,128)(2,1)} %get-tuple-element.43), channel_id=1, replica_groups=mesh['row'=16,'col'=8] {'col'}, dimensions={0}, use_global_device_ids=true | all-gather | bytes 589824 | tf_op jit(solution)/shard_map/all_gather | solution.py:58
  210.7 4.8 fusion.48
  215.6 21.6 %all-gather.7.cloned.1.call-done = bf16[2048,256]{1,0:T(8,128)(2,1)} async-done(((bf16[128,256]{1,0:T(8,128)(2,1)}), bf16[2048,256]{1,0:T(8,128)(2,1)}) %all-gather.7.cloned.1.call-update) | async-done | bytes 1048592 | tf_op jit(solution)/shard_map/all_gather | solution.py:55
  237.2 4.7 fusion.47
  242.1 66.2 %reduce-scatter.15.cloned.1.call-done = f32[128,256]{1,0:T(8,128)} async-done(((f32[2048,256]{1,0:T(8,128)}), f32[128,256]{1,0:T(8,128)}) %reduce-scatter.15.cloned.1.call-update) | async-done | bytes 131088 | tf_op jit(solution)/shard_map/reduce_scatter | solution.py:57
  308.3 39.6 %reduce-scatter.13.cloned.1.call-done = f32[128,256]{1,0:T(8,128)} async-done(((f32[1024,256]{1,0:T(8,128)}), f32[128,256]{1,0:T(8,128)}) %reduce-scatter.13.cloned.1.call-update) | async-done | bytes 131088 | tf_op jit(solution)/shard_map/reduce_scatter | solution.py:45
  347.9 1.6 fusion.39
  349.7 24.2 %all_gather.29 = bf16[1024,256]{1,0:T(8,128)(2,1)S(1)} all-gather(bf16[128,256]{1,0:T(8,128)(2,1)} %get-tuple-element.41), channel_id=1, replica_groups=mesh['row'=16,'col'=8] {'col'}, dimensions={0}, use_global_device_ids=true | all-gather | bytes 589824 | tf_op jit(solution)/shard_map/all_gather | solution.py:58
  373.9 4.8 fusion.50
  378.8 21.2 %all-gather.9.cloned.1.call-done = bf16[2048,256]{1,0:T(8,128)(2,1)} async-done(((bf16[128,256]{1,0:T(8,128)(2,1)}), bf16[2048,256]{1,0:T(8,128)(2,1)}) %all-gather.9.cloned.1.call-update) | async-done | bytes 1048592 | tf_op jit(solution)/shard_map/all_gather | solution.py:55
  400.0 4.7 fusion.49
  405.0 66.3 %reduce-scatter.19.cloned.1.call-done = f32[128,256]{1,0:T(8,128)} async-done(((f32[2048,256]{1,0:T(8,128)}), f32[128,256]{1,0:T(8,128)}) %reduce-scatter.19.cloned.1.call-update) | async-done | bytes 131088 | tf_op jit(solution)/shard_map/reduce_scatter | solution.py:57
  471.3 39.7 %reduce-scatter.17.cloned.1.call-done = f32[128,256]{1,0:T(8,128)} async-done(((f32[1024,256]{1,0:T(8,128)}), f32[128,256]{1,0:T(8,128)}) %reduce-scatter.17.cloned.1.call-update) | async-done | bytes 131088 | tf_op jit(solution)/shard_map/reduce_scatter | solution.py:45
  511.0 1.6 fusion.37
  512.8 24.1 %all_gather.31 = bf16[1024,256]{1,0:T(8,128)(2,1)S(1)} all-gather(bf16[128,256]{1,0:T(8,128)(2,1)} %get-tuple-element.39), channel_id=1, replica_groups=mesh['row'=16,'col'=8] {'col'}, dimensions={0}, use_global_device_ids=true | all-gather | bytes 589824 | tf_op jit(solution)/shard_map/all_gather | solution.py:58
  536.8 4.8 fusion.53
  541.8 21.2 %all-gather.11.cloned.1.call-done = bf16[2048,256]{1,0:T(8,128)(2,1)} async-done(((bf16[128,256]{1,0:T(8,128)(2,1)}), bf16[2048,256]{1,0:T(8,128)(2,1)}) %all-gather.11.cloned.1.call-update) | async-done | bytes 1048592 | tf_op jit(solution)/shard_map/all_gather | solution.py:55
  563.0 4.7 fusion.52
  568.0 0.9 fusion.51
  568.9 65.4 %reduce-scatter.23.cloned.1.call-done = f32[128,256]{1,0:T(8,128)} async-done(((f32[2048,256]{1,0:T(8,128)}), f32[128,256]{1,0:T(8,128)}) %reduce-scatter.23.cloned.1.call-update) | async-done | bytes 131088 | tf_op jit(solution)/shard_map/reduce_scatter | solution.py:57
  634.3 39.6 %reduce-scatter.21.cloned.1.call-done = f32[128,256]{1,0:T(8,128)} async-done(((f32[1024,256]{1,0:T(8,128)}), f32[128,256]{1,0:T(8,128)}) %reduce-scatter.21.cloned.1.call-update) | async-done | bytes 131088 | tf_op jit(solution)/shard_map/reduce_scatter | solution.py:45
  673.9 1.0 fusion.7
  674.9 1.0 fusion.54
  675.9 152.6 %all-reduce.4.cloned.1.call-done = (f32[256,256]{0,1:T(8,128)}, f32[256,256]{1,0:T(8,128)}) async-done(((f32[256,256]{0,1:T(8,128)}, f32[256,256]{1,0:T(8,128)}), (f32[256,256]{0,1:T(8,128)}, f32[256,256]{1,0:T(8,128)})) %all-reduce.4.cloned.1.call-update) | async-done | bytes 524304 | tf_op jit(solution)/shard_map/psum | solution.py:80
  828.6 1.0 broadcast_multiply_fusion
  829.7 1.1 copy.12
  830.8 1.1 fusion.1
  831.9 11.7 %cholesky.50 = f32[128,128]{1,0:T(8,128)S(1)} custom-call(f32[128,128]{1,0:T(8,128)S(1)} %cholesky.118), custom_call_target="Cholesky" | custom-call | tf_op jit(solution)/shard_map/jit(cholesky)/cholesky | solution.py:83
  843.7 9.8 %custom-call.18 = f32[1,128,128]{1,2,0:T(8,128)S(1)} custom-call(f32[1,128,128]{2,1,0:T(8,128)S(1)} %get-tuple-element.50), custom_call_target="InvertDiagBlocksLowerTriangular" | custom-call | tf_op jit(solution)/shard_map/jit(cholesky)/cholesky | solution.py:83
  854.0 11.7 %cholesky.105 = f32[128,128]{1,0:T(8,128)S(1)} custom-call(f32[128,128]{1,0:T(8,128)S(1)} %convolution_subtract_fusion.3), custom_call_target="Cholesky" | custom-call | tf_op jit(solution)/shard_map/jit(cholesky)/cholesky | solution.py:83
  865.7 0.7 compare_reduce_fusion
  866.4 0.6 compare_reduce_fusion.1
  868.5 4.3 while.5
  869.3 1.4 bitcast_dynamic-update-slice_fusion.2
  871.4 1.4 bitcast_dynamic-update-slice_fusion.2
  872.8 19.7 %custom-call.19 = f32[2,128,128]{1,2,0:T(8,128)S(1)} custom-call(f32[2,128,128]{2,1,0:T(8,128)S(1)} %get-tuple-element.18), custom_call_target="InvertDiagBlocksLowerTriangular" | custom-call | tf_op jit(solution)/shard_map/jit(_solve_triangular)/triangular_solve | solution.py:84
  894.4 0.7 pad_maximum_fusion
  896.1 0.8 copy.13
  (75 shorter events, 6.3 us)
Async XLA Ops:
  7.2 8.6 copy-start.7
  7.2 8.7 copy-start.6
  7.2 64.4 %all-gather.5.cloned.1.call-start = ((), (), s32[]{:S(2)}) async-start(), calls=%async_computation.8 | async-start | bytes 1114112 | tf_op jit(solution)/shard_map/all_gather | solution.py:55
  8.8 136.5 %reduce-scatter.11.cloned.1.call-start = ((), (), s32[]{:S(2)}) async-start(), calls=%async_computation.10 | async-start | bytes 2228224 | tf_op jit(solution)/shard_map/reduce_scatter | solution.py:57
  24.7 12.4 %copy-start.2 = (bf16[128,256]{1,0:T(8,128)(2,1)S(1)}, bf16[128,256]{1,0:T(8,128)(2,1)}, u32[]{:S(2)}) copy-start(bf16[128,256]{1,0:T(8,128)(2,1)} %convert_element_type.20) | copy-start | bytes 196612
  71.5 6.2 copy-start.5
  71.5 113.6 %copy-start.1 = (f32[128,256]{1,0:T(8,128)S(1)}, f32[128,256]{1,0:T(8,128)}, u32[]{:S(2)}) copy-start(f32[128,256]{1,0:T(8,128)} %param.9) | copy-start | bytes 393220
  71.5 113.6 %reduce-scatter.9.cloned.1.call-start = ((), (), s32[]{:S(2)}) async-start(), calls=%async_computation.9 | async-start | bytes 1179648 | tf_op jit(solution)/shard_map/reduce_scatter | solution.py:45
  76.3 160.9 %all-gather.7.cloned.1.call-start = ((), (), s32[]{:S(2)}) async-start(), calls=%async_computation.11 | async-start | bytes 1114112 | tf_op jit(solution)/shard_map/all_gather | solution.py:55
  186.7 121.6 %reduce-scatter.15.cloned.1.call-start = ((), (), s32[]{:S(2)}) async-start(), calls=%async_computation.13 | async-start | bytes 2228224 | tf_op jit(solution)/shard_map/reduce_scatter | solution.py:57
  215.5 26.5 %copy-start.3 = (bf16[128,256]{1,0:T(8,128)(2,1)S(1)}, bf16[128,256]{1,0:T(8,128)(2,1)}, u32[]{:S(2)}) copy-start(bf16[128,256]{1,0:T(8,128)(2,1)} %get-tuple-element.43) | copy-start | bytes 196612
  215.5 132.4 %reduce-scatter.13.cloned.1.call-start = ((), (), s32[]{:S(2)}) async-start(), calls=%async_computation.12 | async-start | bytes 1179648 | tf_op jit(solution)/shard_map/reduce_scatter | solution.py:45
  241.9 158.1 %all-gather.9.cloned.1.call-start = ((), (), s32[]{:S(2)}) async-start(), calls=%async_computation.14 | async-start | bytes 1114112 | tf_op jit(solution)/shard_map/all_gather | solution.py:55
  349.6 121.7 %reduce-scatter.19.cloned.1.call-start = ((), (), s32[]{:S(2)}) async-start(), calls=%async_computation.16 | async-start | bytes 2228224 | tf_op jit(solution)/shard_map/reduce_scatter | solution.py:57
  378.7 26.1 %copy-start.4 = (bf16[128,256]{1,0:T(8,128)(2,1)S(1)}, bf16[128,256]{1,0:T(8,128)(2,1)}, u32[]{:S(2)}) copy-start(bf16[128,256]{1,0:T(8,128)(2,1)} %get-tuple-element.41) | copy-start | bytes 196612
  378.7 132.3 %reduce-scatter.17.cloned.1.call-start = ((), (), s32[]{:S(2)}) async-start(), calls=%async_computation.15 | async-start | bytes 1179648 | tf_op jit(solution)/shard_map/reduce_scatter | solution.py:45
  404.8 158.2 %all-gather.11.cloned.1.call-start = ((), (), s32[]{:S(2)}) async-start(), calls=%async_computation.17 | async-start | bytes 1114112 | tf_op jit(solution)/shard_map/all_gather | solution.py:55
  512.7 121.6 %reduce-scatter.23.cloned.1.call-start = ((), (), s32[]{:S(2)}) async-start(), calls=%async_computation.19 | async-start | bytes 2228224 | tf_op jit(solution)/shard_map/reduce_scatter | solution.py:57
  541.7 26.1 %copy-start = (bf16[128,256]{1,0:T(8,128)(2,1)S(1)}, bf16[128,256]{1,0:T(8,128)(2,1)}, u32[]{:S(2)}) copy-start(bf16[128,256]{1,0:T(8,128)(2,1)} %get-tuple-element.39) | copy-start | bytes 196612
  541.7 132.2 %reduce-scatter.21.cloned.1.call-start = ((), (), s32[]{:S(2)}) async-start(), calls=%async_computation.18 | async-start | bytes 1179648 | tf_op jit(solution)/shard_map/reduce_scatter | solution.py:45
  567.8 260.8 %all-reduce.4.cloned.1.call-start = ((), (), s32[]{:S(2)}) async-start(), calls=%async_computation.20 | async-start | bytes 1048576 | tf_op jit(solution)/shard_map/psum | solution.py:80
Sparse Core Ops, SparseCore 0:
  11.0 50.9 all-gather.4
  71.6 73.7 reduce-scatter.10
  147.7 37.2 reduce-scatter.8
  187.9 49.2 all-gather.6
  241.0 67.3 reduce-scatter.14
  310.6 37.3 reduce-scatter.12
  351.0 49.0 all-gather.8
  404.0 67.3 reduce-scatter.18
  473.7 37.2 reduce-scatter.16
  513.9 49.0 all-gather.10
  566.9 67.3 reduce-scatter.22
  636.5 37.3 reduce-scatter.20
  679.4 149.1 all-reduce.3
where the time goes:
time: 904 us; the launch traced here: 903 us
  waiting for transfers between devices  641 us (71%)
  blocking collectives  102 us (11%)
  other arithmetic  64.7 us (7%)
  matrix products  52.9 us (6%)
  local copies, waits for them, and re-layouts  25.5 us (3%)
  between operations  16.8 us (2%)
    reduce_scatter x4, waiting for transfers between devices, apply(): lax.psum_scatter(mirror_rows(dense_tile, lax.all_gather(rounded, 'col', a...  265 us
    reduce_scatter x4, waiting for transfers between devices, reduce_direct(): return lax.psum_scatter(terms, 'col', scatter_dimension=0, tiled=True)  159 us
    psum x1, waiting for transfers between devices, local(): gram_total, cross_total = lax.psum((gram_part, cross_part), ('row', 'col'))  153 us
    all_gather x4, blocking collectives, apply(): lax.all_gather(rounded, 'col', axis=0, tiled=True)  102 us
    all_gather x4, waiting for transfers between devices, apply(): lax.all_gather(rounded, 'row', axis=0, tiled=True)  64.1 us
    another operation x7, other arithmetic, local(): factor = jnp.linalg.cholesky(gram_matrix)  34.7 us
    another operation x3, other arithmetic, local(): jax.scipy.linalg.solve_triangular(factor, current.T, lower=True)  19.7 us
    dot_general x4, matrix products, mirror_rows(): lax.dot_general(dense_tile, row_set, (((0,), (0,)), ((), ())), preferred_...  19.4 us
  transfers between devices with their start and end apart: 13, of which 12 were waited for; matrix products, arithmetic and copies ran while one was open for 8% of the time, Pallas kernels for 0%

commit v1 on v0

--- a/solution.py
+++ b/solution.py
@@ -7,6 +7,11 @@
 K = 256
 PB = 2
 DEG = 3
+
+
+def axis_by_axis(value, one, other):
+    partial = lax.psum(value, one)
+    return lax.psum(partial, other)
 
 
 def add_columns(dense_tile, portion):
@@ -77,7 +82,7 @@
     gram_part = lax.dot_general(rounded, rounded, contract, preferred_element_type=jnp.float32)
     image = apply(rounded)
     cross_part = lax.dot_general(as_float, image, contract, precision=lax.Precision.HIGHEST)
-    gram_total, cross_total = lax.psum((gram_part, cross_part), ("row", "col"))
+    gram_total, cross_total = axis_by_axis((gram_part, cross_part), "col", "row")
     gram_matrix = gram_total / total_rows
     ritz_matrix = (cross_total + cross_total.T) / (2.0 * total_rows)
     factor = jnp.linalg.cholesky(gram_matrix)

time: 904 us -> 973 us (1.076)
  waiting for transfers between devices: 641 us -> 710 us
    psum x1 -> x2, waiting for transfers between devices: 153 us -> 221 us  [the longest x1 145 us: axis_by_axis(): return lax.psum(partial, other)]
  transfers between devices with their start and end apart: 13 -> 14, of which waited for: 12 -> 13; matrix products, arithmetic and copies ran while one was open for 8% -> 7% of each run, Pallas kernels for 0% -> 0%
where the time goes in v1:
time: 973 us; the launch traced here: 972 us
  waiting for transfers between devices  710 us (73%)
  blocking collectives  101 us (10%)
  other arithmetic  64.6 us (7%)
  matrix products  52.8 us (5%)
  local copies, waits for them, and re-layouts  25.4 us (3%)
  between operations  16.8 us (2%)
    reduce_scatter x4, waiting for transfers between devices, apply(): lax.psum_scatter(mirror_rows(dense_tile, lax.all_gather(rounded, 'col', a...  266 us
    reduce_scatter x4, waiting for transfers between devices, reduce_direct(): return lax.psum_scatter(terms, 'col', scatter_dimension=0, tiled=True)  159 us
    psum x1, waiting for transfers between devices, axis_by_axis(): return lax.psum(partial, other)  145 us
    all_gather x4, blocking collectives, apply(): lax.all_gather(rounded, 'col', axis=0, tiled=True)  101 us
    psum x1, waiting for transfers between devices, axis_by_axis(): partial = lax.psum(value, one)  76.2 us
    all_gather x4, waiting for transfers between devices, apply(): lax.all_gather(rounded, 'row', axis=0, tiled=True)  63.8 us
    another operation x7, other arithmetic, local(): factor = jnp.linalg.cholesky(gram_matrix)  34.6 us
    another operation x3, other arithmetic, local(): jax.scipy.linalg.solve_triangular(factor, current.T, lower=True)  19.7 us
  transfers between devices with their start and end apart: 14, of which 13 were waited for; matrix products, arithmetic and copies ran while one was open for 7% of the time, Pallas kernels for 0%

profile of v1, /device:TPU:1, one launch (start us, length us, event | category | flops | bytes accessed | tf_op | source)
XLA Modules:
  0.0 971.7 jit_solution(8816418691415318224)
XLA Ops:
  7.2 1.5 convert_element_type.20
  8.8 6.9 reshape.92
  15.8 8.9 convert_bitcast_fusion
  24.7 12.4 %reshape.93 = bf16[1024,2048]{1,0:T(8,128)(2,1)} reshape(bf16[16,64,32,64]{3,2,1,0:T(8,128)(2,1)} %convert_bitcast_fusion) | data formatting | bytes 8388608 | tf_op jit(solution)/shard_map/reshape | solution.py:37
  37.1 29.0 %all_gather.25 = bf16[1024,256]{1,0:T(8,128)(2,1)S(1)} all-gather(bf16[128,256]{1,0:T(8,128)(2,1)S(1)} %copy-done.2), channel_id=1, replica_groups=mesh['row'=16,'col'=8] {'col'}, dimensions={0}, use_global_device_ids=true | all-gather | bytes 589824 | tf_op jit(solution)/shard_map/all_gather | solution.py:63
  66.1 4.8 fusion.46
  71.1 4.7 fusion.45
  77.4 67.9 %reduce-scatter.11.cloned.1.call-done = f32[128,256]{1,0:T(8,128)} async-done(((f32[2048,256]{1,0:T(8,128)}), f32[128,256]{1,0:T(8,128)}) %reduce-scatter.11.cloned.1.call-update) | async-done | bytes 131088 | tf_op jit(solution)/shard_map/reduce_scatter | solution.py:62
  145.4 39.9 %reduce-scatter.9.cloned.1.call-done = f32[128,256]{1,0:T(8,128)} async-done(((f32[1024,256]{1,0:T(8,128)}), f32[128,256]{1,0:T(8,128)}) %reduce-scatter.9.cloned.1.call-update) | async-done | bytes 131088 | tf_op jit(solution)/shard_map/reduce_scatter | solution.py:50
  185.2 1.6 fusion.41
  186.9 24.0 %all_gather.27 = bf16[1024,256]{1,0:T(8,128)(2,1)S(1)} all-gather(bf16[128,256]{1,0:T(8,128)(2,1)} %get-tuple-element.45), channel_id=1, replica_groups=mesh['row'=16,'col'=8] {'col'}, dimensions={0}, use_global_device_ids=true | all-gather | bytes 589824 | tf_op jit(solution)/shard_map/all_gather | solution.py:63
  210.9 4.8 fusion.48
  215.9 21.3 %all-gather.7.cloned.1.call-done = bf16[2048,256]{1,0:T(8,128)(2,1)} async-done(((bf16[128,256]{1,0:T(8,128)(2,1)}), bf16[2048,256]{1,0:T(8,128)(2,1)}) %all-gather.7.cloned.1.call-update) | async-done | bytes 1048592 | tf_op jit(solution)/shard_map/all_gather | solution.py:60
  237.1 4.7 fusion.47
  242.1 66.2 %reduce-scatter.15.cloned.1.call-done = f32[128,256]{1,0:T(8,128)} async-done(((f32[2048,256]{1,0:T(8,128)}), f32[128,256]{1,0:T(8,128)}) %reduce-scatter.15.cloned.1.call-update) | async-done | bytes 131088 | tf_op jit(solution)/shard_map/reduce_scatter | solution.py:62
  308.3 39.5 %reduce-scatter.13.cloned.1.call-done = f32[128,256]{1,0:T(8,128)} async-done(((f32[1024,256]{1,0:T(8,128)}), f32[128,256]{1,0:T(8,128)}) %reduce-scatter.13.cloned.1.call-update) | async-done | bytes 131088 | tf_op jit(solution)/shard_map/reduce_scatter | solution.py:50
  347.8 1.6 fusion.39
  349.5 24.3 %all_gather.29 = bf16[1024,256]{1,0:T(8,128)(2,1)S(1)} all-gather(bf16[128,256]{1,0:T(8,128)(2,1)} %get-tuple-element.43), channel_id=1, replica_groups=mesh['row'=16,'col'=8] {'col'}, dimensions={0}, use_global_device_ids=true | all-gather | bytes 589824 | tf_op jit(solution)/shard_map/all_gather | solution.py:63
  373.8 4.8 fusion.50
  378.7 21.2 %all-gather.9.cloned.1.call-done = bf16[2048,256]{1,0:T(8,128)(2,1)} async-done(((bf16[128,256]{1,0:T(8,128)(2,1)}), bf16[2048,256]{1,0:T(8,128)(2,1)}) %all-gather.9.cloned.1.call-update) | async-done | bytes 1048592 | tf_op jit(solution)/shard_map/all_gather | solution.py:60
  400.0 4.7 fusion.49
  404.9 66.4 %reduce-scatter.19.cloned.1.call-done = f32[128,256]{1,0:T(8,128)} async-done(((f32[2048,256]{1,0:T(8,128)}), f32[128,256]{1,0:T(8,128)}) %reduce-scatter.19.cloned.1.call-update) | async-done | bytes 131088 | tf_op jit(solution)/shard_map/reduce_scatter | solution.py:62
  471.3 39.7 %reduce-scatter.17.cloned.1.call-done = f32[128,256]{1,0:T(8,128)} async-done(((f32[1024,256]{1,0:T(8,128)}), f32[128,256]{1,0:T(8,128)}) %reduce-scatter.17.cloned.1.call-update) | async-done | bytes 131088 | tf_op jit(solution)/shard_map/reduce_scatter | solution.py:50
  511.0 1.6 fusion.37
  512.7 24.1 %all_gather.31 = bf16[1024,256]{1,0:T(8,128)(2,1)S(1)} all-gather(bf16[128,256]{1,0:T(8,128)(2,1)} %get-tuple-element.41), channel_id=1, replica_groups=mesh['row'=16,'col'=8] {'col'}, dimensions={0}, use_global_device_ids=true | all-gather | bytes 589824 | tf_op jit(solution)/shard_map/all_gather | solution.py:63
  536.8 4.8 fusion.53
  541.7 21.2 %all-gather.11.cloned.1.call-done = bf16[2048,256]{1,0:T(8,128)(2,1)} async-done(((bf16[128,256]{1,0:T(8,128)(2,1)}), bf16[2048,256]{1,0:T(8,128)(2,1)}) %all-gather.11.cloned.1.call-update) | async-done | bytes 1048592 | tf_op jit(solution)/shard_map/all_gather | solution.py:60
  562.9 4.7 fusion.52
  567.9 0.9 fusion.51
  568.8 65.4 %reduce-scatter.23.cloned.1.call-done = f32[128,256]{1,0:T(8,128)} async-done(((f32[2048,256]{1,0:T(8,128)}), f32[128,256]{1,0:T(8,128)}) %reduce-scatter.23.cloned.1.call-update) | async-done | bytes 131088 | tf_op jit(solution)/shard_map/reduce_scatter | solution.py:62
  634.2 39.6 %reduce-scatter.21.cloned.1.call-done = f32[128,256]{1,0:T(8,128)} async-done(((f32[1024,256]{1,0:T(8,128)}), f32[128,256]{1,0:T(8,128)}) %reduce-scatter.21.cloned.1.call-update) | async-done | bytes 131088 | tf_op jit(solution)/shard_map/reduce_scatter | solution.py:50
  673.8 1.0 fusion.7
  674.8 1.0 fusion.54
  675.9 76.2 %all-reduce.8.cloned.1.call-done = (f32[256,256]{0,1:T(8,128)}, f32[256,256]{1,0:T(8,128)}) async-done(((f32[256,256]{0,1:T(8,128)}, f32[256,256]{1,0:T(8,128)}), (f32[256,256]{0,1:T(8,128)}, f32[256,256]{1,0:T(8,128)})) %all-reduce.8.cloned.1.call-update) | async-done | bytes 524304 | tf_op jit(solution)/shard_map/psum | solution.py:13
  752.1 145.0 %all-reduce.6.cloned.1.call-done = (f32[256,256]{0,1:T(8,128)}, f32[256,256]{1,0:T(8,128)}) async-done(((f32[256,256]{0,1:T(8,128)}, f32[256,256]{1,0:T(8,128)}), (f32[256,256]{0,1:T(8,128)}, f32[256,256]{1,0:T(8,128)})) %all-reduce.6.cloned.1.call-update) | async-done | bytes 524304 | tf_op jit(solution)/shard_map/psum | solution.py:14
  897.2 1.0 broadcast_multiply_fusion
  898.3 1.1 copy.12
  899.4 1.1 fusion.1
  900.5 11.7 %cholesky.50 = f32[128,128]{1,0:T(8,128)S(1)} custom-call(f32[128,128]{1,0:T(8,128)S(1)} %cholesky.118), custom_call_target="Cholesky" | custom-call | tf_op jit(solution)/shard_map/jit(cholesky)/cholesky | solution.py:88
  912.3 9.8 %custom-call.18 = f32[1,128,128]{1,2,0:T(8,128)S(1)} custom-call(f32[1,128,128]{2,1,0:T(8,128)S(1)} %get-tuple-element.52), custom_call_target="InvertDiagBlocksLowerTriangular" | custom-call | tf_op jit(solution)/shard_map/jit(cholesky)/cholesky | solution.py:88
  922.5 11.7 %cholesky.105 = f32[128,128]{1,0:T(8,128)S(1)} custom-call(f32[128,128]{1,0:T(8,128)S(1)} %convolution_subtract_fusion.3), custom_call_target="Cholesky" | custom-call | tf_op jit(solution)/shard_map/jit(cholesky)/cholesky | solution.py:88
  934.3 0.7 compare_reduce_fusion
  937.0 4.1 while.5
  937.7 1.4 bitcast_dynamic-update-slice_fusion.2
  939.7 1.4 bitcast_dynamic-update-slice_fusion.2
  941.1 19.7 %custom-call.19 = f32[2,128,128]{1,2,0:T(8,128)S(1)} custom-call(f32[2,128,128]{2,1,0:T(8,128)S(1)} %get-tuple-element.18), custom_call_target="InvertDiagBlocksLowerTriangular" | custom-call | tf_op jit(solution)/shard_map/jit(_solve_triangular)/triangular_solve | solution.py:89
  962.7 0.7 pad_maximum_fusion
  964.4 0.8 copy.13
  (78 shorter events, 7.0 us)
Async XLA Ops:
  7.2 8.6 copy-start.7
  7.2 8.7 copy-start.6
  7.2 63.9 %all-gather.5.cloned.1.call-start = ((), (), s32[]{:S(2)}) async-start(), calls=%async_computation.8 | async-start | bytes 1114112 | tf_op jit(solution)/shard_map/all_gather | solution.py:60
  8.8 136.6 %reduce-scatter.11.cloned.1.call-start = ((), (), s32[]{:S(2)}) async-start(), calls=%async_computation.10 | async-start | bytes 2228224 | tf_op jit(solution)/shard_map/reduce_scatter | solution.py:62
  24.7 12.4 %copy-start.2 = (bf16[128,256]{1,0:T(8,128)(2,1)S(1)}, bf16[128,256]{1,0:T(8,128)(2,1)}, u32[]{:S(2)}) copy-start(bf16[128,256]{1,0:T(8,128)(2,1)} %convert_element_type.20) | copy-start | bytes 196612
  71.0 6.2 copy-start.5
  71.0 114.2 %copy-start.1 = (f32[128,256]{1,0:T(8,128)S(1)}, f32[128,256]{1,0:T(8,128)}, u32[]{:S(2)}) copy-start(f32[128,256]{1,0:T(8,128)} %param.9) | copy-start | bytes 393220
  71.0 114.2 %reduce-scatter.9.cloned.1.call-start = ((), (), s32[]{:S(2)}) async-start(), calls=%async_computation.9 | async-start | bytes 1179648 | tf_op jit(solution)/shard_map/reduce_scatter | solution.py:50
  75.8 161.3 %all-gather.7.cloned.1.call-start = ((), (), s32[]{:S(2)}) async-start(), calls=%async_computation.11 | async-start | bytes 1114112 | tf_op jit(solution)/shard_map/all_gather | solution.py:60
  186.9 121.4 %reduce-scatter.15.cloned.1.call-start = ((), (), s32[]{:S(2)}) async-start(), calls=%async_computation.13 | async-start | bytes 2228224 | tf_op jit(solution)/shard_map/reduce_scatter | solution.py:62
  215.8 26.1 %copy-start.3 = (bf16[128,256]{1,0:T(8,128)(2,1)S(1)}, bf16[128,256]{1,0:T(8,128)(2,1)}, u32[]{:S(2)}) copy-start(bf16[128,256]{1,0:T(8,128)(2,1)} %get-tuple-element.45) | copy-start | bytes 196612
  215.8 132.0 %reduce-scatter.13.cloned.1.call-start = ((), (), s32[]{:S(2)}) async-start(), calls=%async_computation.12 | async-start | bytes 1179648 | tf_op jit(solution)/shard_map/reduce_scatter | solution.py:50
  241.9 158.1 %all-gather.9.cloned.1.call-start = ((), (), s32[]{:S(2)}) async-start(), calls=%async_computation.14 | async-start | bytes 1114112 | tf_op jit(solution)/shard_map/all_gather | solution.py:60
  349.5 121.8 %reduce-scatter.19.cloned.1.call-start = ((), (), s32[]{:S(2)}) async-start(), calls=%async_computation.16 | async-start | bytes 2228224 | tf_op jit(solution)/shard_map/reduce_scatter | solution.py:62
  378.7 26.1 %copy-start.4 = (bf16[128,256]{1,0:T(8,128)(2,1)S(1)}, bf16[128,256]{1,0:T(8,128)(2,1)}, u32[]{:S(2)}) copy-start(bf16[128,256]{1,0:T(8,128)(2,1)} %get-tuple-element.43) | copy-start | bytes 196612
  378.7 132.3 %reduce-scatter.17.cloned.1.call-start = ((), (), s32[]{:S(2)}) async-start(), calls=%async_computation.15 | async-start | bytes 1179648 | tf_op jit(solution)/shard_map/reduce_scatter | solution.py:50
  404.7 158.2 %all-gather.11.cloned.1.call-start = ((), (), s32[]{:S(2)}) async-start(), calls=%async_computation.17 | async-start | bytes 1114112 | tf_op jit(solution)/shard_map/all_gather | solution.py:60
  512.6 121.6 %reduce-scatter.23.cloned.1.call-start = ((), (), s32[]{:S(2)}) async-start(), calls=%async_computation.19 | async-start | bytes 2228224 | tf_op jit(solution)/shard_map/reduce_scatter | solution.py:62
  541.6 26.1 %copy-start = (bf16[128,256]{1,0:T(8,128)(2,1)S(1)}, bf16[128,256]{1,0:T(8,128)(2,1)}, u32[]{:S(2)}) copy-start(bf16[128,256]{1,0:T(8,128)(2,1)} %get-tuple-element.41) | copy-start | bytes 196612
  541.6 132.2 %reduce-scatter.21.cloned.1.call-start = ((), (), s32[]{:S(2)}) async-start(), calls=%async_computation.18 | async-start | bytes 1179648 | tf_op jit(solution)/shard_map/reduce_scatter | solution.py:50
  567.7 184.4 %all-reduce.8.cloned.1.call-start = ((), (), s32[]{:S(2)}) async-start(), calls=%async_computation.21 | async-start | bytes 1048576 | tf_op jit(solution)/shard_map/psum | solution.py:13
  675.9 221.3 %all-reduce.6.cloned.1.call-start = ((), (), s32[]{:S(2)}) async-start(), calls=%async_computation.20 | async-start | bytes 1048576 | tf_op jit(solution)/shard_map/psum | solution.py:14
Sparse Core Ops, SparseCore 0:
  11.0 50.9 all-gather.4
  71.1 74.2 reduce-scatter.10
  147.7 37.4 reduce-scatter.8
  188.1 48.9 all-gather.6
  240.9 67.3 reduce-scatter.14
  310.5 37.2 reduce-scatter.12
  350.8 49.0 all-gather.8
  403.9 67.3 reduce-scatter.18
  473.7 37.2 reduce-scatter.16
  513.9 49.0 all-gather.10
  566.9 67.3 reduce-scatter.22
  636.5 37.3 reduce-scatter.20
  676.9 75.1 all-reduce.7
  754.6 142.5 all-reduce.5
